TPU v7x, 256 devices: a whole 4x4x8 slice. The times are simulated.
256 devices in a mesh: dp: 32 (over x, z_hi, y), ctx: 8 (over z_lo, core).
Axes of the slice: x: 4, y: 4, z: 8 (z_hi: 2, z_lo: 4; z = z_hi * 4 + z_lo), core: 2. Of those that a mesh axis runs over, the one named last changes fastest.
Arguments:
- queries: bfloat16 [32, 2048, 1024], P('dp', 'ctx'), may hold values from -7 to 7
- key_states: bfloat16 [32, 2048, 1024], P('dp', 'ctx'), may hold values from -7 to 7
- value_states: bfloat16 [32, 2048, 1024], P('dp', 'ctx'), may hold values from -6 to 6
- token_order: int32 [32, 2048], P('dp', 'ctx'), may hold values from 0 to 2047, each once within a row
- block_pattern: int32 [32, 16, 4], P('dp'), may hold values from -1 to 15, as said below
- out_weight: bfloat16 [1024, 2048], P('dp'), may hold values from -0.1875 to 0.1875
- out_grad: bfloat16 [32, 2048, 2048], P('dp', 'ctx'), may hold values from -6 to 6
Outputs:
- layer_out: bfloat16 [32, 2048, 2048], P('dp', 'ctx')
- query_grad: bfloat16 [32, 2048, 1024], P('dp', 'ctx')
- key_grad: bfloat16 [32, 2048, 1024], P('dp', 'ctx')
- value_grad: bfloat16 [32, 2048, 1024], P('dp', 'ctx')
- weight_grad: float32 [1024, 2048], P('dp')
Inputs may be any that keep to these rules, and one draw needn't show every extreme that they name: `block_pattern`: row b of a session lists key blocks of the same session, each within 2 blocks of b, none twice; slot 0 holds b itself, used slots come before the slots that hold -1, and a row is full whenever 4 blocks lie within that reach.
All inputs are finite; a program needn't handle non-finite values.
Results may differ from a plain program's by a relative error of at most 0.012.
Values may be sent and summed in bfloat16 or wider, within the bound.
A program may use at most 128 MiB of HBM per device.

v0:
```python
import math

import jax
import jax.numpy as jnp
from jax import lax
from jax.sharding import PartitionSpec as P

H = 8
HD = 128
BLK = 128
KB = 4


def padded(shard, sides, width):
    for axis, dim in sides:
        devices, length = (lax.axis_size(axis), shard.shape[dim])
        up = [(i, (i + 1) % devices) for i in range(devices - 1)]
        down = [(j, i) for i, j in up]
        last = lax.slice_in_dim(shard, length - width, length, axis=dim)
        leading = lax.slice_in_dim(shard, 0, width, axis=dim)
        before = lax.ppermute(last, axis, up)
        after = lax.ppermute(leading, axis, down)
        shard = jnp.concatenate([before, shard, after], axis=dim)
    return shard


def from_behind(block, axis, distance):
    devices = range(lax.axis_size(axis))
    route = [(i - distance, i) for i in devices if i - distance in devices]
    return lax.ppermute(block, axis, route)


def rope_tables(positions):
    coords = jnp.stack(
        [positions % 8, positions // 8 % 8, positions // 64 % 4, positions // 256], axis=1
    ).astype(jnp.float32)
    per_axis = HD // 16
    frequency = 100.0 ** (-jnp.arange(per_axis, dtype=jnp.float32) / per_axis)
    angle = (coords[:, :, None] * frequency[None, None, :]).reshape(
        positions.shape[0], 4 * per_axis
    )
    return (jnp.cos(angle), jnp.sin(angle))


def rotate_heads(heads, cosine, sine_vals, direction):
    quarter = HD // 4
    first_part = heads[..., :quarter]
    second_part = heads[..., quarter : 2 * quarter]
    cos_rows = cosine[:, None, :]
    sin_rows = direction * sine_vals[:, None, :]
    return jnp.concatenate(
        [
            first_part * cos_rows - second_part * sin_rows,
            second_part * cos_rows + first_part * sin_rows,
            heads[..., 2 * quarter :],
        ],
        axis=-1,
    )


def attend_forward(query_blocks, key_sets, value_sets, key_mask, score_scale):
    scores = (
        jnp.einsum("nqhd,nkhd->nhqk", query_blocks, key_sets, preferred_element_type=jnp.float32)
        * score_scale
    )
    scores = jnp.where(key_mask[:, None, None, :], scores, -jnp.inf)
    row_peak = jnp.max(scores, axis=-1)
    row_total = jnp.sum(jnp.exp(scores - row_peak[..., None]), axis=-1)
    log_total = row_peak + jnp.log(row_total)
    soft_probs = jnp.exp(scores - log_total[..., None]).astype(jnp.bfloat16)
    block_out = jnp.einsum(
        "nhqk,nkhd->nqhd", soft_probs, value_sets, preferred_element_type=jnp.float32
    ).astype(jnp.bfloat16)
    return (block_out, log_total)


def attend_backward(
    query_blocks,
    key_sets,
    value_sets,
    key_mask,
    log_total,
    grad_dot,
    grad_blocks,
    score_scale,
    key_form,
):
    scores = (
        jnp.einsum(
            "nqhd," + key_form + "->nhqk",
            query_blocks,
            key_sets,
            preferred_element_type=jnp.float32,
        )
        * score_scale
    )
    scores = jnp.where(key_mask[:, None, None, :], scores, -jnp.inf)
    exact_probs = jnp.exp(scores - log_total[..., None])
    soft_probs = exact_probs.astype(jnp.bfloat16)
    value_part = jnp.einsum(
        "nhqk,nqhd->" + key_form, soft_probs, grad_blocks, preferred_element_type=jnp.float32
    )
    prob_grad = jnp.einsum(
        "nqhd," + key_form + "->nhqk", grad_blocks, value_sets, preferred_element_type=jnp.float32
    )
    score_grad = (exact_probs * (prob_grad - grad_dot[..., None]) * score_scale).astype(
        jnp.bfloat16
    )
    query_part = jnp.einsum(
        "nhqk," + key_form + "->nqhd", score_grad, key_sets, preferred_element_type=jnp.float32
    )
    key_part = jnp.einsum(
        "nhqk,nqhd->" + key_form, score_grad, query_blocks, preferred_element_type=jnp.float32
    )
    return (query_part, key_part, value_part)


def shards(queries, key_states, value_states, token_order, block_pattern, out_weight, out_grad):
    row_count = queries.shape[1]
    feature_width = queries.shape[2]
    local_blocks = row_count // BLK
    shard_index = lax.axis_index("ctx")
    score_scale = 1.0 / math.sqrt(HD)
    cosine, sine_vals = rope_tables(token_order[0])
    rot_query = rotate_heads(
        queries[0].astype(jnp.float32).reshape(row_count, H, HD), cosine, sine_vals, 1.0
    ).astype(jnp.bfloat16)
    rot_keys = rotate_heads(
        key_states[0].astype(jnp.float32).reshape(row_count, H, HD), cosine, sine_vals, 1.0
    ).astype(jnp.bfloat16)
    stacked = jnp.stack([rot_keys.reshape(row_count, feature_width), value_states[0]], axis=1)
    extended = padded(stacked, (("ctx", 0),), row_count)
    ext_blocks = extended.reshape(3 * local_blocks, BLK, 2, H, HD)
    pattern_rows = block_pattern[0]
    first_block = shard_index * local_blocks
    my_pattern = lax.dynamic_slice_in_dim(pattern_rows, first_block, local_blocks, 0)
    slot_valid = my_pattern >= 0
    slot_local = jnp.where(slot_valid, my_pattern - first_block + local_blocks, 0)
    gathered = jnp.take(ext_blocks, slot_local, axis=0)
    key_sets = gathered[:, :, :, 0].reshape(local_blocks, KB * BLK, H, HD)
    value_sets = gathered[:, :, :, 1].reshape(local_blocks, KB * BLK, H, HD)
    key_mask = jnp.repeat(slot_valid, BLK, axis=1)
    query_blocks = rot_query.reshape(local_blocks, BLK, H, HD)
    block_out, log_total = attend_forward(query_blocks, key_sets, value_sets, key_mask, score_scale)
    attn = block_out.reshape(row_count, feature_width)
    grad_rows = out_grad[0]
    forward_weight = lax.all_gather(out_weight, "dp", axis=0, tiled=True)
    layer_out = jnp.dot(attn, forward_weight, preferred_element_type=jnp.float32).astype(
        jnp.bfloat16
    )
    attn_grad = lax.dot_general(
        grad_rows,
        lax.all_gather(out_weight, "dp", axis=0, tiled=True),
        (((1,), (1,)), ((), ())),
        preferred_element_type=jnp.float32,
    ).astype(jnp.bfloat16)
    batch_count = lax.axis_size("dp")
    local_grad = lax.psum_scatter(
        lax.dot_general(
            attn, grad_rows, (((0,), (0,)), ((), ())), preferred_element_type=jnp.float32
        )
        / batch_count,
        "dp",
        scatter_dimension=0,
        tiled=True,
    )
    weight_grad = lax.psum(local_grad, "ctx")
    dot_rows = jnp.sum(
        (attn_grad.astype(jnp.float32) * attn.astype(jnp.float32)).reshape(row_count, H, HD),
        axis=-1,
    )
    grad_dot = dot_rows.reshape(local_blocks, BLK, H).transpose(0, 2, 1)
    grad_blocks = attn_grad.reshape(local_blocks, BLK, H, HD)
    query_part, key_part, value_part = attend_backward(
        query_blocks,
        key_sets,
        value_sets,
        key_mask,
        log_total,
        grad_dot,
        grad_blocks,
        score_scale,
        "nkhd",
    )
    query_grad = (
        rotate_heads(query_part.reshape(row_count, H, HD), cosine, sine_vals, -1.0)
        .reshape(row_count, feature_width)
        .astype(jnp.bfloat16)
    )
    keep = slot_valid.reshape(local_blocks * KB).astype(jnp.float32)[:, None, None, None, None]
    both_parts = (
        jnp.stack(
            [
                key_part.reshape(local_blocks * KB, BLK, H, HD),
                value_part.reshape(local_blocks * KB, BLK, H, HD),
            ],
            axis=2,
        )
        * keep
    )
    accumulated = (
        jnp.zeros((3 * local_blocks, BLK, 2, H, HD), jnp.float32)
        .at[slot_local.reshape(-1)]
        .add(both_parts)
    )
    accumulated = accumulated.reshape(3 * row_count, 2, feature_width)
    own_part = accumulated[row_count : 2 * row_count]
    from_right = from_behind(accumulated[:row_count], "ctx", -1)
    from_left = from_behind(accumulated[2 * row_count :], "ctx", 1)
    summed = own_part + from_right + from_left
    key_total = summed[:, 0]
    value_total = summed[:, 1]
    key_grad = (
        rotate_heads(key_total.reshape(row_count, H, HD), cosine, sine_vals, -1.0)
        .reshape(row_count, feature_width)
        .astype(jnp.bfloat16)
    )
    value_grad = value_total.astype(jnp.bfloat16)
    return (layer_out[None], query_grad[None], key_grad[None], value_grad[None], weight_grad)


def solution(mesh):
    in_specs = (
        P("dp", "ctx", None),
        P("dp", "ctx", None),
        P("dp", "ctx", None),
        P("dp", "ctx"),
        P("dp", None, None),
        P("dp", None),
        P("dp", "ctx", None),
    )
    out_specs = (
        P("dp", "ctx", None),
        P("dp", "ctx", None),
        P("dp", "ctx", None),
        P("dp", "ctx", None),
        P("dp", None),
    )
    return jax.shard_map(shards, mesh=mesh, in_specs=in_specs, out_specs=out_specs, check_vma=False)
```

profile of v0, /device:TPU:1, one launch (start us, length us, event | category | flops | bytes accessed | tf_op | source)
XLA Modules:
  0.0 468.8 jit_solution(280626574308070015)
XLA Ops:
  9.2 1.1 copy.124
  10.3 1.1 copy.121
  11.9 0.7 subtract_convert_fusion.2
  12.7 1.3 pad_maximum_fusion.2
  13.9 1.3 convert_element_type.105
  15.2 2.1 pad_maximum_fusion.1
  17.3 5.1 %collective-permute-start.1 = (bf16[256,2,1024]{2,0,1:T(8,128)(2,1)}, bf16[256,2,1024]{2,0,1:T(8,128)(2,1)}, u32[]{:S(2)}, u32[]{:S(2)}) collective-permute-start(bf16[256,2,1024]{2,0,1:T(8,128)(2,1)} %pad_maximum_fusion.1), channel_id=1, source_target_pairs={{1,0},{2,1},{3,2},{4,3},{5,4},{6,5},{7,6},{9,8},{10,9},{11,10},{12... | collective-permute-start | bytes 3145736 | tf_op jit(solution)/shard_map/ppermute | solution.py:22
  22.5 2.1 collective-permute-start
  25.4 0.9 copy.91
  26.3 0.9 copy.89
  27.2 0.9 copy.90
  28.1 9.0 %collective-permute-done.1 = bf16[256,2,1024]{2,0,1:T(8,128)(2,1)} collective-permute-done((bf16[256,2,1024]{2,0,1:T(8,128)(2,1)}, bf16[256,2,1024]{2,0,1:T(8,128)(2,1)}, u32[]{:S(2)}, u32[]{:S(2)}) %collective-permute-start.1) | collective-permute-done | bytes 1048608 | tf_op jit(solution)/shard_map/ppermute | solution.py:22
  37.2 1.1 collective-permute-done
  38.3 1.8 pad_maximum_fusion
  40.1 0.8 copy.122
  40.9 2.2 copy.111
  43.1 4.9 %gather_fusion = bf16[8,128,2,8,128]{4,3,2,1,0:T(8,128)(2,1)} fusion(bf16[6,128,2,8,128]{4,3,2,1,0:T(8,128)(2,1)} %copy.111, s32[1024]{0:T(1024)S(1)} %pad_clamp_fusion), kind=kCustom, calls=%fused_computation | custom fusion | bytes 8388640 | tf_op jit(solution)/shard_map/jit(_take)/gather | solution.py:139
  48.0 2.7 broadcast_select_fusion
  50.7 2.1 fusion.27
  53.3 4.3 copy.112
  57.6 2.6 fusion.1
  60.3 1.3 exponential_reduce_fusion
  62.2 1.9 fusion.4
  64.2 2.1 copy.93
  66.3 5.6 %convolution_multiply_fusion = f32[1024,2048]{1,0:T(8,128)} fusion(bf16[1,256,2048]{2,1,0:T(8,128)(2,1)S(1)} %copy-done, bf16[32,8,8,128]{3,2,1,0:T(8,128)(2,1)} %bitcast.146), kind=kOutput, calls=%fused_computation.3 | convolution fusion | flops 1075838976 | bytes 9961472 | tf_op jit(solution)/shard_map/dot_general | solution.py:159
  72.5 50.5 %all-gather.2.cloned.1.call-done = bf16[1024,2048]{1,0:T(8,128)(2,1)} async-done(((bf16[32,2048]{1,0:T(8,128)(2,1)}), bf16[1024,2048]{1,0:T(8,128)(2,1)}) %all-gather.2.cloned.1.call-update) | async-done | bytes 4194320 | tf_op jit(solution)/shard_map/all_gather | solution.py:147
  123.0 3.5 convolution_convert_fusion.1
  126.5 0.8 copy-done.13
  127.4 1.1 copy.102
  128.5 1.4 multiply_bitcast_fusion
  129.9 1.2 copy.127
  131.0 1.6 reduce_sum.19
  132.7 5.5 %convolution_bitcast_fusion = f32[2,512,8,128]{1,3,2,0:T(8,128)} fusion(bf16[2,128,8,128]{1,3,2,0:T(8,128)(2,1)} %copy.102, f32[2,8,128,512]{3,2,1,0:T(8,128)} %copy-done.2, f32[2,8,128]{2,1,0:T(8,128)S(1)} %log_add_fusion, pred[2,512]{1,0:T(4,128)(4,1)S(1)} %bitcast.164), kind=kOutput, calls=%fused_computation.14 | convolution fusion | flops 272629760 | bytes 8922112 | tf_op jit(solution)/shard_map/nhqk,nqhd->nkhd/dot_general | solution.py:100
  138.2 5.2 %copy.103 = f32[2,512,8,128]{3,2,1,0:T(8,128)} copy(f32[2,512,8,128]{1,3,2,0:T(8,128)} %convolution_bitcast_fusion) | data formatting | bytes 8388608 | tf_op jit(solution)/shard_map/nhqk,nqhd->nkhd/transpose | solution.py:100
  143.4 4.7 %multiply_convert_fusion = bf16[2,8,128,512]{3,2,1,0:T(8,128)(2,1)S(1)} fusion(f32[2,8,128,512]{3,2,1,0:T(8,128)} %copy-done.2, bf16[2,128,8,128]{1,3,2,0:T(8,128)(2,1)} %copy.102, bf16[2,512,8,128]{1,3,2,0:T(8,128)(2,1)} %copy.112, f32[2,8,128]{2,1,0:T(8,128)S(1)} %bitcast.166, f32[2,8,128]{2,1,0:T(8,128)S(1)} %log_add_fusion, pred[2,512]{1,0:T(4,128)(4,1)S(1)} %bitcast.165), kind=kOutput, calls=%fused_computation.4 | convolution fusion | flops 275775488 | bytes 8930304 | tf_op jit(solution)/shard_map/nqhd,nkhd->nhqk/dot_general | solution.py:103
  148.2 1.3 copy-done.3
  149.5 3.0 convolution_bitcast_fusion.1
  152.5 5.3 %copy.101 = f32[2,512,8,128]{3,2,1,0:T(8,128)} copy(f32[2,512,8,128]{1,3,2,0:T(8,128)} %convolution_bitcast_fusion.1) | data formatting | bytes 8388608 | tf_op jit(solution)/shard_map/nhqk,nqhd->nkhd/transpose | solution.py:112
  157.9 4.7 %maximum_multiply_fusion = f32[8,128,2,8,128]{4,3,1,0,2:T(8,128)S(1)} fusion(f32[8,128,1,8,128]{4,3,1,0,2:T(8,128)} %bitcast.136, f32[8,128,1,8,128]{4,3,1,0,2:T(8,128)} %bitcast.137, f32[8]{0:T(128)S(1)} %reshape.587), kind=kLoop, calls=%fused_computation.2 | loop fusion | flops 4194304 | bytes 16777248 | tf_op jit(solution)/shard_map/mul | solution.py:192
  162.6 4.0 copy.105
  166.5 3.2 broadcast_in_dim.65
  169.7 17.6 %scatter_fusion = f32[6,128,2,8,128]{4,3,2,1,0:T(8,128)} fusion(f32[6,128,2,8,128]{4,3,2,1,0:T(8,128)} %broadcast_in_dim.65, s32[8]{0:T(128)S(1)} %fusion.19, f32[8,128,2,8,128]{4,3,2,1,0:T(8,128)} %copy.105), kind=kCustom, calls=%fused_computation.1 | custom fusion | flops 2097152 | bytes 25165856 | tf_op jit(solution)/shard_map/scatter-add | solution.py:204
  187.3 5.6 %fusion.26 = (f32[2,128,2,8,128]{4,3,2,1,0:T(8,128)}, f32[2,128,2,8,128]{4,3,2,1,0:T(8,128)}, f32[2,128,2,8,128]{4,3,2,1,0:T(8,128)}) fusion(f32[6,128,2,8,128]{4,3,2,1,0:T(8,128)} %scatter_fusion), kind=kLoop, calls=%fused_computation.96 | loop fusion | bytes 12582912 | tf_op jit(solution)/shard_map/slice | solution.py:207
  192.9 3.2 slice.87
  196.2 3.6 copy.108
  199.8 3.2 slice.85
  203.0 3.6 copy.106
  206.6 6.8 %collective-permute-start.2 = (f32[256,2,1024]{2,0,1:T(8,128)}, f32[256,2,1024]{2,0,1:T(8,128)}, u32[]{:S(2)}, u32[]{:S(2)}) collective-permute-start(f32[256,2,1024]{2,0,1:T(8,128)} %copy.106), channel_id=1, source_target_pairs={{1,0},{2,1},{3,2},{4,3},{5,4},{6,5},{7,6},{9,8},{10,9},{11,10},{12... | collective-permute-start | bytes 6291464 | tf_op jit(solution)/shard_map/ppermute | solution.py:30
  213.4 2.7 collective-permute-start.3
  216.3 2.3 convolution_bitcast_fusion.2
  219.2 1.0 slice.137
  220.2 3.3 slice.83
  223.5 4.6 fusion.2
  228.1 56.4 %collective-permute-done.2 = f32[256,2,1024]{2,0,1:T(8,128)} collective-permute-done((f32[256,2,1024]{2,0,1:T(8,128)}, f32[256,2,1024]{2,0,1:T(8,128)}, u32[]{:S(2)}, u32[]{:S(2)}) %collective-permute-start.2) | collective-permute-done | bytes 2097184 | tf_op jit(solution)/shard_map/ppermute | solution.py:30
  284.8 3.2 fusion.3
  288.3 1.0 slice.136
  289.3 0.7 subtract_convert_fusion
  290.5 1.0 convert_element_type.116
  291.6 1.5 pad_maximum_fusion.5
  293.1 1.0 convert_element_type.119
  294.1 83.3 %reduce-scatter.2.cloned.1.call-done = f32[32,2048]{1,0:T(8,128)} async-done(((f32[1024,2048]{1,0:T(8,128)}), f32[32,2048]{1,0:T(8,128)}) %reduce-scatter.2.cloned.1.call-update) | async-done | bytes 262160 | tf_op jit(solution)/shard_map/reduce_scatter | solution.py:158
  377.5 2.1 fusion.7
  379.6 81.0 %all-reduce.2.cloned.1.call-done = f32[32,2048]{1,0:T(8,128)} async-done(((f32[32,2048]{1,0:T(8,128)}), f32[32,2048]{1,0:T(8,128)}) %all-reduce.2.cloned.1.call-update) | async-done | bytes 262160 | tf_op jit(solution)/shard_map/psum | solution.py:167
  460.6 1.7 copy.145
  (70 shorter events, 6.9 us)
Async XLA Ops:
  7.2 59.1 %copy-start = (bf16[1,256,2048]{2,1,0:T(8,128)(2,1)S(1)}, bf16[1,256,2048]{2,1,0:T(8,128)(2,1)}, u32[]{:S(2)}) copy-start(bf16[1,256,2048]{2,1,0:T(8,128)(2,1)} %param.13) | copy-start | bytes 3145732
  7.2 115.8 %all-gather.2.cloned.1.call-start = ((), (), s32[]{:S(2)}) async-start(), calls=%async_computation.1 | async-start | bytes 4325376 | tf_op jit(solution)/shard_map/all_gather | solution.py:147
  7.9 369.5 %reduce-scatter.2.cloned.1.call-start = ((), (), s32[]{:S(2)}) async-start(), calls=%async_computation.2 | async-start | bytes 8650752 | tf_op jit(solution)/shard_map/reduce_scatter | solution.py:158
  12.6 11.9 %copy-start.14 = (s32[1,16,4]{1,2,0:T(4,128)S(1)}, s32[1,16,4]{1,2,0:T(4,128)}, u32[]{:S(2)}) copy-start(s32[1,16,4]{1,2,0:T(4,128)} %param.11) | copy-start | bytes 772
  17.3 19.9 %collective-permute-start.1 = (bf16[256,2,1024]{2,0,1:T(8,128)(2,1)}, bf16[256,2,1024]{2,0,1:T(8,128)(2,1)}, u32[]{:S(2)}, u32[]{:S(2)}) collective-permute-start(bf16[256,2,1024]{2,0,1:T(8,128)(2,1)} %pad_maximum_fusion.1), channel_id=1, source_target_pairs={{1,0},{2,1},{3,2},{4,3},{5,4},{6,5},{7,6},{9,8},{10,9},{11,10},{12... | collective-permute-start | bytes 3145736 | tf_op jit(solution)/shard_map/ppermute | solution.py:22
  22.5 15.8 %collective-permute-start = (bf16[256,2,1024]{2,0,1:T(8,128)(2,1)}, bf16[256,2,1024]{2,0,1:T(8,128)(2,1)}, u32[]{:S(2)}, u32[]{:S(2)}) collective-permute-start(bf16[256,2,1024]{2,0,1:T(8,128)(2,1)} %pad_maximum_fusion.1), channel_id=1, source_target_pairs={{0,1},{1,2},{2,3},{3,4},{4,5},{5,6},{6,7},{8,9},{9,10},{10,11},{11... | collective-permute-start | bytes 3145736 | tf_op jit(solution)/shard_map/ppermute | solution.py:21
  25.2 13.1 %copy-start.11 = (bf16[1,256,1024]{2,1,0:T(8,128)(2,1)S(1)}, bf16[1,256,1024]{2,1,0:T(8,128)(2,1)}, u32[]{:S(2)}) copy-start(bf16[1,256,1024]{2,1,0:T(8,128)(2,1)} %param.9) | copy-start | bytes 1572868
  57.6 4.6 copy-start.10
  60.2 2.0 copy-start.2
  71.9 388.6 %all-reduce.2.cloned.1.call-start = ((), (), s32[]{:S(2)}) async-start(), calls=%async_computation.3 | async-start | bytes 524288 | tf_op jit(solution)/shard_map/psum | solution.py:167
  126.5 0.8 copy-start.13
  143.4 6.1 %copy-start.7 = (bf16[2,128,8,64]{3,1,2,0:T(8,128)(2,1)S(1)}, bf16[2,128,8,64]{3,1,2,0:T(8,128)(2,1)}, u32[]{:S(2)}) copy-start(bf16[2,128,8,64]{3,1,2,0:T(8,128)(2,1)} %copy.91) | copy-start | bytes 786436
  143.4 6.1 %copy-start.8 = (bf16[2,128,8,32]{3,1,2,0:T(8,128)(2,1)S(1)}, bf16[2,128,8,32]{3,1,2,0:T(8,128)(2,1)}, u32[]{:S(2)}) copy-start(bf16[2,128,8,32]{3,1,2,0:T(8,128)(2,1)} %copy.89) | copy-start | bytes 393220
  143.4 6.1 %copy-start.9 = (bf16[2,128,8,32]{3,1,2,0:T(8,128)(2,1)S(1)}, bf16[2,128,8,32]{3,1,2,0:T(8,128)(2,1)}, u32[]{:S(2)}) copy-start(bf16[2,128,8,32]{3,1,2,0:T(8,128)(2,1)} %copy.90) | copy-start | bytes 393220
  148.2 1.3 copy-start.3
  206.6 77.8 %collective-permute-start.2 = (f32[256,2,1024]{2,0,1:T(8,128)}, f32[256,2,1024]{2,0,1:T(8,128)}, u32[]{:S(2)}, u32[]{:S(2)}) collective-permute-start(f32[256,2,1024]{2,0,1:T(8,128)} %copy.106), channel_id=1, source_target_pairs={{1,0},{2,1},{3,2},{4,3},{5,4},{6,5},{7,6},{9,8},{10,9},{11,10},{12... | collective-permute-start | bytes 6291464 | tf_op jit(solution)/shard_map/ppermute | solution.py:30
  213.4 71.4 %collective-permute-start.3 = (f32[256,2,1024]{2,0,1:T(8,128)}, f32[256,2,1024]{2,0,1:T(8,128)}, u32[]{:S(2)}, u32[]{:S(2)}) collective-permute-start(f32[256,2,1024]{2,0,1:T(8,128)} %copy.108), channel_id=1, source_target_pairs={{0,1},{1,2},{2,3},{3,4},{4,5},{5,6},{6,7},{8,9},{9,10},{10,11},{11... | collective-permute-start | bytes 6291464 | tf_op jit(solution)/shard_map/ppermute | solution.py:30
  218.6 4.9 %copy-start.6 = (bf16[2,128,8,128]{3,2,1,0:T(8,128)(2,1)S(1)}, bf16[2,128,8,128]{3,2,1,0:T(8,128)(2,1)}, u32[]{:S(2)}) copy-start(bf16[2,128,8,128]{3,2,1,0:T(8,128)(2,1)} %copy.93) | copy-start | bytes 1572868
  223.5 61.3 %copy-start.4 = (f32[256,2,1024]{2,1,0:T(2,128)S(1)}, f32[256,2,1024]{2,1,0:T(2,128)}, u32[]{:S(2)}) copy-start(f32[256,2,1024]{2,1,0:T(2,128)} %slice.83) | copy-start | bytes 6291460
  288.0 2.0 copy-start.5
  288.3 1.8 copy-start.12
  289.3 173.0 %copy-start.1 = (bf16[1,256,2048]{2,1,0:T(8,128)(2,1)S(1)}, bf16[1,256,2048]{2,1,0:T(8,128)(2,1)}, u32[]{:S(2)}) copy-start(bf16[1,256,2048]{2,1,0:T(8,128)(2,1)} %param.13) | copy-start | bytes 3145732
Sparse Core Ops, SparseCore 0:
  11.5 111.4 all-gather.1
  125.6 251.8 reduce-scatter.1
  380.1 80.4 all-reduce.1
where the time goes:
time: 472 us; the launch traced here: 469 us
  waiting for transfers between devices  282 us (60%)
  local copies, waits for them, and re-layouts  79 us (17%)
  other arithmetic  42.3 us (9%)
  matrix products  33.8 us (7%)
  starting transfers between devices  17.1 us (4%)
  between operations  14.1 us (3%)
    reduce_scatter x1, waiting for transfers between devices, shards(): lax.psum_scatter(lax.dot_general(attn, grad_rows, (((0,), (0,)), ((), ())...  83.3 us
    psum x1, waiting for transfers between devices, shards(): weight_grad = lax.psum(local_grad, 'ctx')  81 us
    ppermute x2, waiting for transfers between devices, from_behind(): return lax.ppermute(block, axis, route)  56.8 us
    all_gather x1, waiting for transfers between devices, shards(): forward_weight = lax.all_gather(out_weight, 'dp', axis=0, tiled=True)  50.5 us
    scatter-add x1, other arithmetic, shards(): accumulated = jnp.zeros((3 * local_blocks, BLK, 2, H, HD), jnp.float32).a...  17.6 us
    ppermute x2, starting transfers between devices, from_behind(): return lax.ppermute(block, axis, route)  9.52 us
  transfers between devices with their start and end apart: 7, of which 7 were waited for; matrix products, arithmetic and copies ran while one was open for 32% of the time, Pallas kernels for 0%

commit v1 on v0

v1 whole, which is shorter than its diff:
```python
import functools
import math

import jax
import jax.numpy as jnp
from jax import lax
from jax.experimental import pallas as pl
from jax.experimental.pallas import tpu as pltpu
from jax.sharding import PartitionSpec as P

MESH = pl.DeviceIdType.MESH
F32 = jnp.float32
BF16 = jnp.bfloat16
H = 8
HD = 128
BLK = 128
KB = 4
T = 256
NK = 3 * T
D = 2048
HALF = D // 2
ROWS = 32
SCALE = 1.0 / math.sqrt(HD)
NT = (((1,), (1,)), ((), ()))
TN = (((0,), (0,)), ((), ()))
NEG = -1e30


def dot(a, b, dims=(((1,), (0,)), ((), ()))):
    return lax.dot_general(a, b, dims, preferred_element_type=F32)


def rcopy(src, dst, send, recv, device):
    return pltpu.make_async_remote_copy(
        src_ref=src, dst_ref=dst, send_sem=send, recv_sem=recv, device_id=device, device_id_type=MESH
    )


class Gather:
    def __init__(self, unit, pos, f, device, send, recv):
        self.unit = lambda step: unit(lax.rem(pos + step * f + 8, 4))
        self.to = lambda step: device(lax.rem(pos + step * f + 8, 4))
        self.send, self.recv = send, recv

    def copy(self, step, slot, to):
        u = self.unit(step)
        return rcopy(u, u, self.send.at[slot], self.recv.at[slot], self.to(to))

    def start(self):
        self.copy(0, 0, 1).start()
        self.copy(0, 1, -1).start()

    def forward(self):
        self.copy(-1, 0, 1).wait_recv()
        self.copy(-1, 2, 1).start()

    def near(self):
        self.copy(1, 1, -1).wait_recv()

    def far(self):
        self.copy(2, 2, 1).wait_recv()

    def drain(self):
        self.copy(0, 0, 1).wait_send()
        self.copy(0, 1, -1).wait_send()
        self.copy(-1, 2, 1).wait_send()


class Scatter:
    def __init__(self, chunk, pos, f, device, send, recv, bufs):
        self.chunk = lambda step: chunk(lax.rem(pos + step * f + 8, 4))
        self.to = lambda step: device(lax.rem(pos + step * f + 8, 4))
        self.send, self.recv, self.bufs = send, recv, bufs

    def copy(self, src, slot, to):
        return rcopy(src, self.bufs.at[slot], self.send.at[slot], self.recv.at[slot], self.to(to))

    def start(self):
        self.copy(self.chunk(2), 0, 1).start()
        self.copy(self.chunk(-1), 1, -1).start()

    def middle(self):
        self.copy(self.bufs.at[0], 0, 1).wait_recv()
        self.bufs[3] = (self.bufs[0].astype(F32) + self.chunk(1)[...].astype(F32)).astype(BF16)
        self.copy(self.bufs.at[3], 2, 1).start()

    def total(self):
        self.copy(self.bufs.at[1], 1, -1).wait_recv()
        self.copy(self.bufs.at[2], 2, 1).wait_recv()
        return self.chunk(0)[...].astype(F32) + self.bufs[1].astype(F32) + self.bufs[2].astype(F32)

    def drain(self):
        self.copy(self.chunk(2), 0, 1).wait_send()
        self.copy(self.chunk(-1), 1, -1).wait_send()
        self.copy(self.bufs.at[3], 2, 1).wait_send()


def kernel(
    q_hbm, k_hbm, v_hbm, tok_ref, pat_ref, w_hbm, og_hbm,
    lo_hbm, qg_hbm, kg_hbm, vg_hbm, wg_hbm,
    kin, qrot, kv, og, ogs, wb, attn, attns, probs, mask, tabs,
    ret, got, own, qg, kg, vg, lo,
    wg, b1a, b1b, r1a, r1b, b2, zs, zr, fin,
    in_sem, out_sem, halo_s, halo_r, ret_s, ret_r, sib_s, sib_r, wz_s, wz_r,
    ag_s, ag_r, wsib_s, wsib_r, rs_s, rs_r, z_s, z_r, fin_s, fin_r,
):
    dp = lax.axis_index("dp")
    ctx = lax.axis_index("ctx")
    x, zh, y = dp // 8, lax.rem(dp // 4, 2), lax.rem(dp, 4)
    zl, core = ctx // 2, lax.rem(ctx, 2)
    z = zh * 4 + zl
    line = z * 2 + core
    f = 1 - 2 * core

    def device(x_, z_, y_, core_):
        return (x_ * 8 + (z_ // 4) * 4 + y_, lax.rem(z_, 4) * 2 + core_)

    def on_line(at):
        return device(x, at // 2, y, lax.rem(at, 2))

    left, right = on_line(lax.rem(line + 15, 16)), on_line(lax.rem(line + 1, 16))
    sibling = (dp, ctx + f)
    on_x = lambda at: device(at, z, y, core)
    on_y = lambda at: device(x, z, at, core)

    def head_cols(h):
        return pl.ds(h * HD, HD)

    ins = []

    def load(src, dst, sem):
        c = pltpu.make_async_copy(src, dst, in_sem.at[sem])
        c.start()
        return c

    my_half = pl.ds(pl.multiple_of(core * HALF, HALF), HALF)
    in_w = load(w_hbm.at[:, my_half], wb.at[x, zh, y, core], 0)
    in_k = [load(k_hbm.at[:, head_cols(h)], kin.at[h], 1 + h) for h in range(H)]
    in_v = [load(v_hbm.at[:, head_cols(h)], kv.at[h, 1, 1], 9 + h) for h in range(H)]
    in_og = load(og_hbm, og, 17)
    in_q = [load(q_hbm.at[:, head_cols(h)], qrot.at[h], 18 + h) for h in range(H)]

    barrier = pltpu.get_barrier_semaphore()
    for step in range(1, 16):
        pl.semaphore_signal(barrier, inc=1, device_id=on_line(lax.rem(line + step, 16)), device_id_type=MESH)
    for step in (1, 3):
        pl.semaphore_signal(barrier, inc=1, device_id=on_x(lax.rem(x + step, 4)), device_id_type=MESH)
        pl.semaphore_signal(barrier, inc=1, device_id=on_y(lax.rem(y + step, 4)), device_id_type=MESH)

    lane8 = lax.broadcasted_iota(jnp.int32, (8, HD), 1)
    value = lax.broadcasted_iota(jnp.int32, (8, HD), 0).astype(F32)
    freq = jnp.exp(lax.rem(lane8, 8).astype(F32) * (-math.log(100.0) / 8.0))
    cos_of, sin_of = jnp.cos(value * freq), jnp.sin(value * freq)
    tok = jnp.transpose(jnp.broadcast_to(tok_ref[...].astype(F32), (HD, T))).astype(jnp.int32)
    lane = lax.broadcasted_iota(jnp.int32, (T, HD), 1)
    axis = lax.rem(lane, 32) // 8
    shift = jnp.where(axis < 3, axis * 3, 8)
    coord = lax.shift_right_logical(tok, shift) & jnp.where(axis == 2, 3, 7)

    def look_up(table):
        rows = [table[i : i + 1, :] for i in range(8)]
        for bit in range(3):
            on = (coord & (1 << bit)) != 0
            rows = [jnp.where(on, rows[2 * i + 1], rows[2 * i]) for i in range(len(rows) // 2)]
        return rows[0]

    sine = look_up(sin_of)
    tabs[0] = jnp.where(lane < 64, look_up(cos_of), 1.0)
    tabs[1] = jnp.where(lane < 32, -sine, 0.0)
    tabs[2] = jnp.where((lane >= 32) & (lane < 64), sine, 0.0)

    def rotate(v, sign):
        side = pltpu.roll(v, 96, 1) * tabs[1] + pltpu.roll(v, 32, 1) * tabs[2]
        return v * tabs[0] + side if sign > 0 else v * tabs[0] - side

    for i in range(2):
        b = ctx * 2 + i
        for r in range(6):
            kb = ctx * 2 - 2 + r
            hit = (pat_ref[b, 0] == kb) | (pat_ref[b, 1] == kb) | (pat_ref[b, 2] == kb) | (pat_ref[b, 3] == kb)
            fill = jnp.where(hit & (kb >= 0), 0.0, NEG)
            mask[pl.ds(i * BLK, BLK), pl.ds(r * BLK, BLK)] = jnp.full((BLK, BLK), fill, F32)

    in_w.wait()
    pl.semaphore_wait(barrier, 19)

    wz = rcopy(wb.at[x, zh, y, core], wb.at[x, zh, y, core], wz_s, wz_r, device(x, 7 - z, y, core))
    wz.start()
    gathers = []
    for s in range(2):
        half = zh if s == 0 else 1 - zh
        top, bottom = pl.ds(0, 16), pl.ds(16, 16)
        first = (
            Gather(lambda p, half=half, top=top: wb.at[x, half, p, core, top], y, f, on_y, ag_s.at[s, 0], ag_r.at[s, 0]),
            Gather(lambda p, half=half, bottom=bottom: wb.at[p, half, y, core, bottom], x, f, on_x, ag_s.at[s, 1], ag_r.at[s, 1]),
        )
        second = (
            Gather(lambda p, half=half, top=top: wb.at[p, half, :, core, top], x, f, on_x, ag_s.at[s, 2], ag_r.at[s, 2]),
            Gather(lambda p, half=half, bottom=bottom: wb.at[:, half, p, core, bottom], y, f, on_y, ag_s.at[s, 3], ag_r.at[s, 3]),
        )
        gathers.append((first, second))

    def share(s, step, who=None):
        half = zh if s == 0 else 1 - zh
        at = core if who is None else who
        px, py = lax.rem(x + step * f + 8, 4), lax.rem(y + step * f + 8, 4)
        a = wb.at[px, half, :, at, pl.ds(0, 16)]
        c = wb.at[:, half, py, at, pl.ds(16, 16)]
        k = step % 4
        return (
            rcopy(a, a, wsib_s.at[s, 0, k], wsib_r.at[s, 0, k], sibling),
            rcopy(c, c, wsib_s.at[s, 1, k], wsib_r.at[s, 1, k], sibling),
        )

    def send_share(s, step):
        for c in share(s, step):
            c.start()

    for g in gathers[0][0]:
        g.start()

    def halo(h):
        return (
            rcopy(kv.at[h, 1], kv.at[h, 2], halo_s.at[0, h], halo_r.at[0, h], left),
            rcopy(kv.at[h, 1], kv.at[h, 0], halo_s.at[1, h], halo_r.at[1, h], right),
        )

    for h in range(H):
        in_k[h].wait()
        kv[h, 1, 0] = rotate(kin[h].astype(F32), 1).astype(BF16)
        in_v[h].wait()
        if h:
            for c in halo(h - 1):
                c.start()
    in_og.wait()
    for c in halo(H - 1):
        c.start()
    other_half = pl.ds(pl.multiple_of((1 - core) * HALF, HALF), HALF)
    ogc = rcopy(og.at[:, other_half], ogs, sib_s.at[8], sib_r.at[8], sibling)
    ogc.start()

    def attn_copy(h):
        return rcopy(attn.at[h], attns.at[h], sib_s.at[h], sib_r.at[h], sibling)

    for h in range(H):
        in_q[h].wait()
        qrot[h] = rotate(qrot[h].astype(F32), 1).astype(BF16)

    for g in gathers[0][0]:
        g.forward()
    wz.wait_recv()
    for g in gathers[1][0]:
        g.start()

    def second_ring(s):
        for g in gathers[s][0]:
            g.near()
            g.far()
        for g in gathers[s][1]:
            g.start()
        send_share(s, 0)

    second_ring(0)

    def keys(h):
        return kv[h, :, 0].reshape(NK, HD)

    def values(h):
        return kv[h, :, 1].reshape(NK, HD)

    def forward(h, carry):
        for c in halo(h):
            c.wait_recv()
        scores = dot(qrot[h], keys(h), NT) * SCALE + mask[...]
        e = jnp.exp(scores - jnp.max(scores, axis=1, keepdims=True))
        p = (e * (1.0 / jnp.sum(e, axis=1, keepdims=True))).astype(BF16)
        probs[h] = p
        attn[h] = dot(p, values(h)).astype(BF16)

        @pl.when(h == 1)
        def _():
            for g in gathers[1][0]:
                g.forward()

        @pl.when(h == 2)
        def _():
            second_ring(1)

        @pl.when(h == 4)
        def _():
            for g in gathers[0][1]:
                g.forward()
            send_share(0, -1)
            for g in gathers[0][1]:
                g.near()
            send_share(0, 1)

        @pl.when(h == 6)
        def _():
            for g in gathers[1][1]:
                g.forward()
            send_share(1, -1)
            for g in gathers[1][1]:
                g.near()
            send_share(1, 1)

        attn_copy(h).start()
        return carry

    lax.fori_loop(0, H, forward, 0)
    for s in range(2):
        for g in gathers[s][1]:
            g.far()
        send_share(s, 2)

    ogc.wait_recv()

    def weight_term(h, carry):
        attn_copy(h).wait_recv()
        term = dot(attn[h], og[:, my_half], TN) + dot(attns[h], ogs[...], TN)
        wg[h // 2, lax.rem(h, 2)] = (term * (1.0 / 32.0)).astype(BF16).reshape(4, ROWS, HALF)
        return carry

    lax.fori_loop(0, H, weight_term, 0)

    scatters = []
    for s in range(2):
        scatters.append((
            Scatter(lambda p, s=s: wg.at[p, s, :, pl.ds(0, 16)], x, f, on_x, rs_s.at[s, 0], rs_r.at[s, 0], b1a.at[s]),
            Scatter(lambda p, s=s: wg.at[:, s, p, pl.ds(16, 16)], y, f, on_y, rs_s.at[s, 1], rs_r.at[s, 1], b1b.at[s]),
            Scatter(lambda p, s=s: r1a.at[s, p], y, f, on_y, rs_s.at[s, 2], rs_r.at[s, 2], b2.at[s, 0]),
            Scatter(lambda p, s=s: r1b.at[s, p], x, f, on_x, rs_s.at[s, 3], rs_r.at[s, 3], b2.at[s, 1]),
        ))
    for s in range(2):
        scatters[s][0].start()
        scatters[s][1].start()

    for s in range(2):
        for k in range(4):
            step = k if k < 3 else -1
            for c in share(s, step, 1 - core):
                c.wait_recv()

    def give_back(h):
        return (
            rcopy(ret.at[0, h], got.at[1, h], ret_s.at[0, h], ret_r.at[1, h], left),
            rcopy(ret.at[1, h], got.at[0, h], ret_s.at[1, h], ret_r.at[0, h], right),
        )

    def take_back(h):
        return (
            rcopy(ret.at[0, h], got.at[1, h], ret_s.at[0, h], ret_r.at[1, h], right),
            rcopy(ret.at[1, h], got.at[0, h], ret_s.at[1, h], ret_r.at[0, h], left),
        )

    def backward(h, carry):
        w = wb.at[h // 2, lax.rem(h, 2)]
        grad = (
            dot(og[:, :HALF], w[:, 0].reshape(HD, HALF), NT) + dot(og[:, HALF:], w[:, 1].reshape(HD, HALF), NT)
        ).astype(BF16)
        delta = jnp.sum(grad.astype(F32) * attn[h].astype(F32), axis=1, keepdims=True)
        p = probs[h]
        dv = dot(p, grad, TN)
        ret[0, h, 1] = dv[:T].astype(BF16)
        own[h, 1] = dv[T : 2 * T]
        ret[1, h, 1] = dv[2 * T :].astype(BF16)
        ds = (p.astype(F32) * ((dot(grad, values(h), NT) - delta) * SCALE)).astype(BF16)
        dk = dot(ds, qrot[h], TN)
        ret[0, h, 0] = dk[:T].astype(BF16)
        own[h, 0] = dk[T : 2 * T]
        ret[1, h, 0] = dk[2 * T :].astype(BF16)
        qg[h] = rotate(dot(ds, keys(h)), -1).astype(BF16)
        for c in give_back(h):
            c.start()

        @pl.when(h == 3)
        def _():
            for s in range(2):
                scatters[s][0].middle()
                scatters[s][1].middle()

        return carry

    lax.fori_loop(0, H, backward, 0)

    outs = []

    def store(src, dst, sem):
        c = pltpu.make_async_copy(src, dst, out_sem.at[sem])
        c.start()
        outs.append(c)

    for h in range(H):
        store(qg.at[h], qg_hbm.at[:, head_cols(h)], h)

    def reduce_plane():
        for s in range(2):
            r1a[s] = scatters[s][0].total().astype(BF16)
            scatters[s][2].start()
            r1b[s] = scatters[s][1].total().astype(BF16)
            scatters[s][3].start()

    reduce_plane()
    for s in range(2):
        scatters[s][2].middle()
        scatters[s][3].middle()

    rows = jnp.concatenate([attn[h] for h in range(H)], axis=1)

    def project(j, carry):
        cols = pl.ds(pl.multiple_of(lax.rem(j, 4) * 256, 256), 256)
        w = wb[:, :, :, j // 4, :, cols].reshape(H * HD, 256)
        lo[:, pl.ds(pl.multiple_of(j * 256, 256), 256)] = dot(rows, w).astype(BF16)
        return carry

    lax.fori_loop(0, 8, project, 0)
    store(lo, lo_hbm, 8)

    for s in range(2):
        for part in range(2):
            done = scatters[s][2 + part].total().astype(BF16)
            for j in range(4):
                zs[s * 4 + j, pl.ds(part * 16, 16)] = done[:, j * 256 : (j + 1) * 256]

    def z_copy(step):
        to = lax.rem(z + step, 8)
        return rcopy(zs.at[to], zr.at[step - 1], z_s.at[step - 1], z_r.at[step - 1], device(x, to, y, core))

    for step in range(1, 8):
        z_copy(step).start()

    def finish(h, carry):
        for c in take_back(h):
            c.wait_recv()
        dk = own[h, 0] + got[0, h, 0].astype(F32) + got[1, h, 0].astype(F32)
        dv = own[h, 1] + got[0, h, 1].astype(F32) + got[1, h, 1].astype(F32)
        kg[h] = rotate(dk, -1).astype(BF16)
        vg[h] = dv.astype(BF16)
        return carry

    lax.fori_loop(0, H, finish, 0)
    for h in range(H):
        store(kg.at[h], kg_hbm.at[:, head_cols(h)], 9 + h)
        store(vg.at[h], vg_hbm.at[:, head_cols(h)], 17 + h)

    for step in range(1, 8):
        z_copy(step).wait_recv()
    total = zs[z].astype(F32)
    for step in range(7):
        total = total + zr[step].astype(F32)
    fin[ctx] = total

    def fin_copy(step):
        to = lax.rem(ctx + step, 8)
        return rcopy(fin.at[ctx], fin.at[ctx], fin_s.at[step - 1], fin_r.at[step - 1], (dp, to))

    def fin_from(step):
        who = lax.rem(ctx + 8 - step, 8)
        return rcopy(fin.at[who], fin.at[who], fin_s.at[step - 1], fin_r.at[step - 1], (dp, who))

    for step in range(1, 8):
        fin_copy(step).start()
    for step in range(1, 8):
        fin_from(step).wait_recv()
    for c in range(8):
        store(fin.at[c], wg_hbm.at[:, pl.ds((c % 2) * HALF + (c // 2) * 256, 256)], 25 + c)

    wz.wait_send()
    ogc.wait_send()
    for h in range(H):
        attn_copy(h).wait_send()
        for c in (*halo(h), *give_back(h)):
            c.wait_send()
    for s in range(2):
        for g in (*gathers[s][0], *gathers[s][1], *scatters[s]):
            g.drain()
        for k in range(4):
            for c in share(s, k if k < 3 else -1):
                c.wait_send()
    for step in range(1, 8):
        z_copy(step).wait_send()
        fin_copy(step).wait_send()
    for c in outs:
        c.wait()


def shards(queries, key_states, value_states, token_order, block_pattern, out_weight, out_grad):
    any_ = pl.BlockSpec(memory_space=pl.ANY)
    vmem = pl.BlockSpec(memory_space=pltpu.VMEM)
    smem = pl.BlockSpec(memory_space=pltpu.SMEM)
    dma = pltpu.SemaphoreType.DMA
    V = pltpu.VMEM
    token_rows = jax.ShapeDtypeStruct((T, H * HD), BF16)
    out = pl.pallas_call(
        kernel,
        out_shape=(
            jax.ShapeDtypeStruct((T, D), BF16),
            token_rows,
            token_rows,
            token_rows,
            jax.ShapeDtypeStruct((ROWS, D), F32),
        ),
        in_specs=[any_, any_, any_, vmem, smem, any_, any_],
        out_specs=(any_,) * 5,
        scratch_shapes=[
            V((H, T, HD), BF16),
            V((H, T, HD), BF16),
            V((H, 3, 2, T, HD), BF16),
            V((T, D), BF16),
            V((T, HALF), BF16),
            V((4, 2, 4, 2, ROWS, HALF), BF16),
            V((H, T, HD), BF16),
            V((H, T, HD), BF16),
            V((H, T, NK), BF16),
            V((T, NK), F32),
            V((3, T, HD), F32),
            V((2, H, 2, T, HD), BF16),
            V((2, H, 2, T, HD), BF16),
            V((H, 2, T, HD), F32),
            V((H, T, HD), BF16),
            V((H, T, HD), BF16),
            V((H, T, HD), BF16),
            V((T, D), BF16),
            V((4, 2, 4, ROWS, HALF), BF16),
            V((2, 4, 4, 16, HALF), BF16),
            V((2, 4, 4, 16, HALF), BF16),
            V((2, 4, 16, HALF), BF16),
            V((2, 4, 16, HALF), BF16),
            V((2, 2, 4, 16, HALF), BF16),
            V((8, ROWS, 256), BF16),
            V((7, ROWS, 256), BF16),
            V((8, ROWS, 256), F32),
            dma((26,)), dma((33,)),
            dma((2, H)), dma((2, H)), dma((2, H)), dma((2, H)),
            dma((9,)), dma((9,)), dma(()), dma(()),
            dma((2, 4, 3)), dma((2, 4, 3)), dma((2, 2, 4)), dma((2, 2, 4)),
            dma((2, 4, 3)), dma((2, 4, 3)), dma((7,)), dma((7,)), dma((7,)), dma((7,)),
        ],
        compiler_params=pltpu.CompilerParams(
            collective_id=0, has_side_effects=True, vmem_limit_bytes=60 * 1024 * 1024
        ),
    )(
        queries[0], key_states[0], value_states[0], token_order, block_pattern[0], out_weight, out_grad[0]
    )
    lo, qg, kg, vg, wg = out
    return lo[None], qg[None], kg[None], vg[None], wg


def solution(mesh):
    rows = P("dp", "ctx", None)
    in_specs = (rows, rows, rows, P("dp", "ctx"), P("dp", None, None), P("dp", None), rows)
    out_specs = (rows, rows, rows, rows, P("dp", None))
    return jax.shard_map(shards, mesh=mesh, in_specs=in_specs, out_specs=out_specs, check_vma=False)
```

time: 472 us -> 78.1 us (0.17)
  waiting for transfers between devices: 282 us -> 0 us
  local copies, waits for them, and re-layouts: 79 us -> 7.97 us
  Pallas kernels: 0 us -> 69.1 us
  other arithmetic: 42.3 us -> 0 us
  matrix products: 33.8 us -> 0 us
  starting transfers between devices: 17.1 us -> 0 us
  between operations: 14.1 us -> 0.66 us
    reduce_scatter x1 -> x0, waiting for transfers between devices: 83.3 us -> none  [shards(): lax.psum_scatter(lax.dot_general(attn, grad_rows, (((0,), (0,)), ((), ())...]
    psum x1 -> x0, waiting for transfers between devices: 81 us -> none  [shards(): weight_grad = lax.psum(local_grad, 'ctx')]
    pallas_call x0 -> x1, Pallas kernels: none -> 69.1 us  [shards(): pl.pallas_call(kernel, out_shape=(jax.ShapeDtypeStruct((T, D), BF16), tok...]
    ppermute x4 -> x0, waiting for transfers between devices: 66.9 us -> none  [the longest x2 56.8 us: from_behind(): return lax.ppermute(block, axis, route)]
    all_gather x1 -> x0, waiting for transfers between devices: 50.5 us -> none  [shards(): forward_weight = lax.all_gather(out_weight, 'dp', axis=0, tiled=True)]
    dot_general x9 -> x0, matrix products: 33.8 us -> none  [the longest x1 5.62 us: shards(): lax.dot_general(attn, grad_rows, (((0,), (0,)), ((), ())), preferred_elem...]
    slice x12 -> x0, local copies, waits for them, and re-layouts: 27.6 us -> none  [the longest x2 8.9 us: shards(): own_part = accumulated[row_count:2 * row_count]]
    scatter-add x1 -> x0, other arithmetic: 17.6 us -> none  [shards(): accumulated = jnp.zeros((3 * local_blocks, BLK, 2, H, HD), jnp.float32).a...]
  transfers between devices with their start and end apart: 7 -> 0, of which waited for: 7 -> 0; matrix products, arithmetic and copies ran while one was open for 32% -> 0% of each run, Pallas kernels for 0% -> 0%
where the time goes in v1:
time: 78.1 us; the launch traced here: 77.8 us
  Pallas kernels  69.1 us (88%)
  local copies, waits for them, and re-layouts  7.97 us (10%)
    pallas_call x1, Pallas kernels, shards(): pl.pallas_call(kernel, out_shape=(jax.ShapeDtypeStruct((T, D), BF16), tok...  69.1 us
    unnamed x15, local copies, waits for them, and re-layouts  7.29 us

profile of v1, /device:TPU:1, one launch (start us, length us, event | category | flops | bytes accessed | tf_op | source)
XLA Modules:
  0.0 77.8 jit_solution(12070112158477051413)
XLA Ops:
  0.6 0.0 copy-start.4
  0.6 0.7 copy-done.4
  1.3 0.7 copy.12.pat_ref
  2.0 69.1 %shard_map.110 = (bf16[256,2048]{1,0:T(8,128)(2,1)}, bf16[256,1024]{1,0:T(8,128)(2,1)}, bf16[256,1024]{1,0:T(8,128)(2,1)}, bf16[256,1024]{1,0:T(8,128)(2,1)}, f32[32,2048]{1,0:T(8,128)}) custom-call(bf16[256,1024]{1,0:T(8,128)(2,1)} %bitcast.11, bf16[256,1024]{1,0:T(8,128)(2,1)} %bitcast.12, bf16[256,1024]{1,0:T(8,128)(2,1)} %bitcast.13, s32[1,256]{1,0:T(1,128)} %tok_ref.1, ...), custom_call_target="tpu_custom_call" | custom-call | tf_op jit(solution)/shard_map/pallas_call | solution.py:494
  71.1 0.0 copy-start.2
  71.2 2.4 %copy.18 = bf16[1,256,2048]{2,1,0:T(8,128)(2,1)} copy(bf16[1,256,2048]{2,1,0:T(8,128)(2,1)} %bitcast.10) | data formatting | bytes 2097152
  73.5 0.0 copy-done.2
  73.5 0.0 copy-start.1
  73.5 0.8 %copy.19 = bf16[1,256,1024]{2,1,0:T(8,128)(2,1)} copy(bf16[1,256,1024]{2,1,0:T(8,128)(2,1)S(1)} %bitcast.16) | data formatting | bytes 1048576
  74.3 0.4 copy-done.1
  74.8 0.0 copy-start
  74.8 0.8 %copy.20 = bf16[1,256,1024]{2,1,0:T(8,128)(2,1)} copy(bf16[1,256,1024]{2,1,0:T(8,128)(2,1)S(1)} %bitcast.15) | data formatting | bytes 1048576
  75.5 0.4 copy-done
  76.0 0.0 copy-start.3
  76.0 0.8 %copy.21 = bf16[1,256,1024]{2,1,0:T(8,128)(2,1)} copy(bf16[1,256,1024]{2,1,0:T(8,128)(2,1)S(1)} %bitcast.14) | data formatting | bytes 1048576
  76.8 0.3 copy-done.3
  77.1 0.7 copy.22
Async XLA Ops:
  0.6 0.7 copy-start.4
  71.1 2.4 %copy-start.2 = (bf16[256,1024]{1,0:T(8,128)(2,1)S(1)}, bf16[256,1024]{1,0:T(8,128)(2,1)}, u32[]{:S(2)}) copy-start(bf16[256,1024]{1,0:T(8,128)(2,1)} %get-tuple-element.11) | copy-start | bytes 1572868
  73.5 1.2 %copy-start.1 = (bf16[256,1024]{1,0:T(8,128)(2,1)S(1)}, bf16[256,1024]{1,0:T(8,128)(2,1)}, u32[]{:S(2)}) copy-start(bf16[256,1024]{1,0:T(8,128)(2,1)} %get-tuple-element.12) | copy-start | bytes 1572868
  74.8 1.2 %copy-start = (bf16[256,1024]{1,0:T(8,128)(2,1)S(1)}, bf16[256,1024]{1,0:T(8,128)(2,1)}, u32[]{:S(2)}) copy-start(bf16[256,1024]{1,0:T(8,128)(2,1)} %get-tuple-element.13) | copy-start | bytes 1572868
  76.0 1.1 %copy-start.3 = (f32[32,2048]{1,0:T(8,128)S(1)}, f32[32,2048]{1,0:T(8,128)}, u32[]{:S(2)}) copy-start(f32[32,2048]{1,0:T(8,128)} %get-tuple-element.24) | copy-start | bytes 786436

commit v2 on v1

--- a/solution.py
+++ b/solution.py
@@ -24,6 +24,7 @@
 NT = (((1,), (1,)), ((), ()))
 TN = (((0,), (0,)), ((), ()))
 NEG = -1e30
+LIMIT = 40 * 1024 * 1024
 
 
 def dot(a, b, dims=(((1,), (0,)), ((), ()))):
@@ -97,11 +98,11 @@
 
 def kernel(
     q_hbm, k_hbm, v_hbm, tok_ref, pat_ref, w_hbm, og_hbm,
-    lo_hbm, qg_hbm, kg_hbm, vg_hbm, wg_hbm,
+    lo, qg, kg, vg, fin,
     kin, qrot, kv, og, ogs, wb, attn, attns, probs, mask, tabs,
-    ret, got, own, qg, kg, vg, lo,
-    wg, b1a, b1b, r1a, r1b, b2, zs, zr, fin,
-    in_sem, out_sem, halo_s, halo_r, ret_s, ret_r, sib_s, sib_r, wz_s, wz_r,
+    ret, got, own,
+    wg, b1a, b1b, r1a, r1b, b2, zs, zr,
+    in_sem, halo_s, halo_r, ret_s, ret_r, sib_s, sib_r, wz_s, wz_r,
     ag_s, ag_r, wsib_s, wsib_r, rs_s, rs_r, z_s, z_r, fin_s, fin_r,
 ):
     dp = lax.axis_index("dp")
@@ -177,7 +178,7 @@
         b = ctx * 2 + i
         for r in range(6):
             kb = ctx * 2 - 2 + r
-            hit = (pat_ref[b, 0] == kb) | (pat_ref[b, 1] == kb) | (pat_ref[b, 2] == kb) | (pat_ref[b, 3] == kb)
+            hit = (pat_ref[0, b] == kb) | (pat_ref[1, b] == kb) | (pat_ref[2, b] == kb) | (pat_ref[3, b] == kb)
             fill = jnp.where(hit & (kb >= 0), 0.0, NEG)
             mask[pl.ds(i * BLK, BLK), pl.ds(r * BLK, BLK)] = jnp.full((BLK, BLK), fill, F32)
 
@@ -268,25 +269,31 @@
     def values(h):
         return kv[h, :, 1].reshape(NK, HD)
 
-    def forward(h, carry):
-        for c in halo(h):
-            c.wait_recv()
-        scores = dot(qrot[h], keys(h), NT) * SCALE + mask[...]
-        e = jnp.exp(scores - jnp.max(scores, axis=1, keepdims=True))
-        p = (e * (1.0 / jnp.sum(e, axis=1, keepdims=True))).astype(BF16)
-        probs[h] = p
-        attn[h] = dot(p, values(h)).astype(BF16)
-
-        @pl.when(h == 1)
+    def forward(i, carry):
+        heads = [2 * i, 2 * i + 1]
+        for h in heads:
+            for c in halo(h):
+                c.wait_recv()
+        done = []
+        for h in heads:
+            scores = dot(qrot[h], keys(h), NT) * SCALE + mask[...]
+            e = jnp.exp(scores - jnp.max(scores, axis=1, keepdims=True))
+            p = (e * (1.0 / jnp.sum(e, axis=1, keepdims=True))).astype(BF16)
+            done.append((p, dot(p, values(h)).astype(BF16)))
+        for h, (p, a) in zip(heads, done):
+            probs[h] = p
+            attn[h] = a
+
+        @pl.when(i == 0)
         def _():
             for g in gathers[1][0]:
                 g.forward()
 
-        @pl.when(h == 2)
+        @pl.when(i == 1)
         def _():
             second_ring(1)
 
-        @pl.when(h == 4)
+        @pl.when(i == 2)
         def _():
             for g in gathers[0][1]:
                 g.forward()
@@ -295,7 +302,7 @@
                 g.near()
             send_share(0, 1)
 
-        @pl.when(h == 6)
+        @pl.when(i == 3)
         def _():
             for g in gathers[1][1]:
                 g.forward()
@@ -304,10 +311,11 @@
                 g.near()
             send_share(1, 1)
 
-        attn_copy(h).start()
+        for h in heads:
+            attn_copy(h).start()
         return carry
 
-    lax.fori_loop(0, H, forward, 0)
+    lax.fori_loop(0, H // 2, forward, 0)
     for s in range(2):
         for g in gathers[s][1]:
             g.far()
@@ -353,57 +361,54 @@
             rcopy(ret.at[1, h], got.at[0, h], ret_s.at[1, h], ret_r.at[0, h], left),
         )
 
-    def backward(h, carry):
-        w = wb.at[h // 2, lax.rem(h, 2)]
-        grad = (
-            dot(og[:, :HALF], w[:, 0].reshape(HD, HALF), NT) + dot(og[:, HALF:], w[:, 1].reshape(HD, HALF), NT)
+    def reduce_plane(s):
+        r1a[s] = scatters[s][0].total().astype(BF16)
+        scatters[s][2].start()
+        r1b[s] = scatters[s][1].total().astype(BF16)
+        scatters[s][3].start()
+
+    def middle(s, ring):
+        for part in range(2):
+            scatters[s][2 * ring + part].middle()
+
+    def backward(i, carry):
+        w = wb.at[i]
+        heads = [2 * i, 2 * i + 1]
+        grads = (
+            dot(og[:, :HALF], w[:, :, 0].reshape(2 * HD, HALF), NT)
+            + dot(og[:, HALF:], w[:, :, 1].reshape(2 * HD, HALF), NT)
         ).astype(BF16)
-        delta = jnp.sum(grad.astype(F32) * attn[h].astype(F32), axis=1, keepdims=True)
-        p = probs[h]
-        dv = dot(p, grad, TN)
-        ret[0, h, 1] = dv[:T].astype(BF16)
-        own[h, 1] = dv[T : 2 * T]
-        ret[1, h, 1] = dv[2 * T :].astype(BF16)
-        ds = (p.astype(F32) * ((dot(grad, values(h), NT) - delta) * SCALE)).astype(BF16)
-        dk = dot(ds, qrot[h], TN)
-        ret[0, h, 0] = dk[:T].astype(BF16)
-        own[h, 0] = dk[T : 2 * T]
-        ret[1, h, 0] = dk[2 * T :].astype(BF16)
-        qg[h] = rotate(dot(ds, keys(h)), -1).astype(BF16)
-        for c in give_back(h):
-            c.start()
-
-        @pl.when(h == 3)
+        done = []
+        for n, h in enumerate(heads):
+            grad = grads[:, n * HD : (n + 1) * HD]
+            delta = jnp.sum(grad.astype(F32) * attn[h].astype(F32), axis=1, keepdims=True)
+            p = probs[h]
+            dv = dot(p, grad, TN)
+            ds = (p.astype(F32) * ((dot(grad, values(h), NT) - delta) * SCALE)).astype(BF16)
+            dk = dot(ds, qrot[h], TN)
+            done.append((dv, dk, rotate(dot(ds, keys(h)), -1).astype(BF16)))
+        for h, (dv, dk, dq) in zip(heads, done):
+            ret[0, h, 1] = dv[:T].astype(BF16)
+            own[h, 1] = dv[T : 2 * T]
+            ret[1, h, 1] = dv[2 * T :].astype(BF16)
+            ret[0, h, 0] = dk[:T].astype(BF16)
+            own[h, 0] = dk[T : 2 * T]
+            ret[1, h, 0] = dk[2 * T :].astype(BF16)
+            qg[h] = dq
+        for h in heads:
+            for c in give_back(h):
+                c.start()
+
+        @pl.when(i == 2)
         def _():
-            for s in range(2):
-                scatters[s][0].middle()
-                scatters[s][1].middle()
+            middle(0, 0)
+            middle(1, 0)
 
         return carry
 
-    lax.fori_loop(0, H, backward, 0)
-
-    outs = []
-
-    def store(src, dst, sem):
-        c = pltpu.make_async_copy(src, dst, out_sem.at[sem])
-        c.start()
-        outs.append(c)
-
-    for h in range(H):
-        store(qg.at[h], qg_hbm.at[:, head_cols(h)], h)
-
-    def reduce_plane():
-        for s in range(2):
-            r1a[s] = scatters[s][0].total().astype(BF16)
-            scatters[s][2].start()
-            r1b[s] = scatters[s][1].total().astype(BF16)
-            scatters[s][3].start()
-
-    reduce_plane()
-    for s in range(2):
-        scatters[s][2].middle()
-        scatters[s][3].middle()
+    lax.fori_loop(0, H // 2, backward, 0)
+    reduce_plane(0)
+    reduce_plane(1)
 
     rows = jnp.concatenate([attn[h] for h in range(H)], axis=1)
 
@@ -411,10 +416,15 @@
         cols = pl.ds(pl.multiple_of(lax.rem(j, 4) * 256, 256), 256)
         w = wb[:, :, :, j // 4, :, cols].reshape(H * HD, 256)
         lo[:, pl.ds(pl.multiple_of(j * 256, 256), 256)] = dot(rows, w).astype(BF16)
+
+        @pl.when(j == 3)
+        def _():
+            middle(0, 1)
+            middle(1, 1)
+
         return carry
 
     lax.fori_loop(0, 8, project, 0)
-    store(lo, lo_hbm, 8)
 
     for s in range(2):
         for part in range(2):
@@ -439,10 +449,6 @@
         return carry
 
     lax.fori_loop(0, H, finish, 0)
-    for h in range(H):
-        store(kg.at[h], kg_hbm.at[:, head_cols(h)], 9 + h)
-        store(vg.at[h], vg_hbm.at[:, head_cols(h)], 17 + h)
-
     for step in range(1, 8):
         z_copy(step).wait_recv()
     total = zs[z].astype(F32)
@@ -462,8 +468,6 @@
         fin_copy(step).start()
     for step in range(1, 8):
         fin_from(step).wait_recv()
-    for c in range(8):
-        store(fin.at[c], wg_hbm.at[:, pl.ds((c % 2) * HALF + (c // 2) * 256, 256)], 25 + c)
 
     wz.wait_send()
     ogc.wait_send()
@@ -480,12 +484,26 @@
     for step in range(1, 8):
         z_copy(step).wait_send()
         fin_copy(step).wait_send()
-    for c in outs:
+
+
+def write(lo, qg, kg, vg, fin, lo_hbm, qg_hbm, kg_hbm, vg_hbm, wg_hbm, sem):
+    copies = [(lo, lo_hbm)]
+    for h in range(H):
+        cols = pl.ds(h * HD, HD)
+        for src, dst in ((qg, qg_hbm), (kg, kg_hbm), (vg, vg_hbm)):
+            copies.append((src.at[h], dst.at[:, cols]))
+    for c in range(8):
+        copies.append((fin.at[c], wg_hbm.at[:, pl.ds((c % 2) * HALF + (c // 2) * 256, 256)]))
+    copies = [pltpu.make_async_copy(src, dst, sem.at[i]) for i, (src, dst) in enumerate(copies)]
+    for c in copies:
+        c.start()
+    for c in copies:
         c.wait()
 
 
 def shards(queries, key_states, value_states, token_order, block_pattern, out_weight, out_grad):
     any_ = pl.BlockSpec(memory_space=pl.ANY)
+    hbm = lambda array: pltpu.with_memory_space_constraint(array, pltpu.HBM)
     vmem = pl.BlockSpec(memory_space=pltpu.VMEM)
     smem = pl.BlockSpec(memory_space=pltpu.SMEM)
     dma = pltpu.SemaphoreType.DMA
@@ -494,14 +512,14 @@
     out = pl.pallas_call(
         kernel,
         out_shape=(
-            jax.ShapeDtypeStruct((T, D), BF16),
-            token_rows,
-            token_rows,
-            token_rows,
-            jax.ShapeDtypeStruct((ROWS, D), F32),
+            V((T, D), BF16),
+            V((H, T, HD), BF16),
+            V((H, T, HD), BF16),
+            V((H, T, HD), BF16),
+            V((8, ROWS, 256), F32),
         ),
         in_specs=[any_, any_, any_, vmem, smem, any_, any_],
-        out_specs=(any_,) * 5,
+        out_specs=(vmem,) * 5,
         scratch_shapes=[
             V((H, T, HD), BF16),
             V((H, T, HD), BF16),
@@ -517,10 +535,6 @@
             V((2, H, 2, T, HD), BF16),
             V((2, H, 2, T, HD), BF16),
             V((H, 2, T, HD), F32),
-            V((H, T, HD), BF16),
-            V((H, T, HD), BF16),
-            V((H, T, HD), BF16),
-            V((T, D), BF16),
             V((4, 2, 4, ROWS, HALF), BF16),
             V((2, 4, 4, 16, HALF), BF16),
             V((2, 4, 4, 16, HALF), BF16),
@@ -529,20 +543,38 @@
             V((2, 2, 4, 16, HALF), BF16),
             V((8, ROWS, 256), BF16),
             V((7, ROWS, 256), BF16),
-            V((8, ROWS, 256), F32),
-            dma((26,)), dma((33,)),
+            dma((26,)),
             dma((2, H)), dma((2, H)), dma((2, H)), dma((2, H)),
             dma((9,)), dma((9,)), dma(()), dma(()),
             dma((2, 4, 3)), dma((2, 4, 3)), dma((2, 2, 4)), dma((2, 2, 4)),
             dma((2, 4, 3)), dma((2, 4, 3)), dma((7,)), dma((7,)), dma((7,)), dma((7,)),
         ],
         compiler_params=pltpu.CompilerParams(
-            collective_id=0, has_side_effects=True, vmem_limit_bytes=60 * 1024 * 1024
+            collective_id=0, has_side_effects=True, vmem_limit_bytes=LIMIT
         ),
     )(
-        queries[0], key_states[0], value_states[0], token_order, block_pattern[0], out_weight, out_grad[0]
+        hbm(queries[0]),
+        hbm(key_states[0]),
+        hbm(value_states[0]),
+        token_order,
+        jnp.transpose(block_pattern[0]),
+        hbm(out_weight),
+        hbm(out_grad[0]),
     )
-    lo, qg, kg, vg, wg = out
+    lo, qg, kg, vg, wg = pl.pallas_call(
+        write,
+        out_shape=(
+            jax.ShapeDtypeStruct((T, D), BF16),
+            token_rows,
+            token_rows,
+            token_rows,
+            jax.ShapeDtypeStruct((ROWS, D), F32),
+        ),
+        in_specs=[vmem] * 5,
+        out_specs=(any_,) * 5,
+        scratch_shapes=[dma((33,))],
+        compiler_params=pltpu.CompilerParams(vmem_limit_bytes=LIMIT),
+    )(*(pltpu.with_memory_space_constraint(o, pltpu.VMEM) for o in out))
     return lo[None], qg[None], kg[None], vg[None], wg
 
 

time: 78.1 us -> 69.5 us (0.89)
  local copies, waits for them, and re-layouts: 7.97 us -> 0.68 us
  Pallas kernels: 69.1 us -> 68.1 us
    unnamed x15 -> x4, local copies, waits for them, and re-layouts: 7.29 us -> 0.68 us
    pallas_call x1 -> x2, Pallas kernels: 69.1 us -> 68.1 us  [the longest x1 66.2 us: shards(): pl.pallas_call(kernel, out_shape=(V((T, D), BF16), V((H, T, HD), BF16), V...]
where the time goes in v2:
time: 69.5 us; the launch traced here: 69.4 us
  Pallas kernels  68.1 us (98%)
    pallas_call x1, Pallas kernels, shards(): pl.pallas_call(kernel, out_shape=(V((T, D), BF16), V((H, T, HD), BF16), V...  66.2 us
    pallas_call x1, Pallas kernels, shards(): pl.pallas_call(write, out_shape=(jax.ShapeDtypeStruct((T, D), BF16), toke...  1.84 us

profile of v2, /device:TPU:1, one launch (start us, length us, event | category | flops | bytes accessed | tf_op | source)
XLA Modules:
  0.0 69.4 jit_solution(10885231842362902341)
XLA Ops:
  0.6 0.0 copy-start
  0.6 0.0 copy-start.1
  0.7 0.7 copy-done
  1.3 0.0 copy-done.1
  1.3 66.2 %shard_map.110 = (bf16[256,2048]{1,0:T(8,128)(2,1)S(1)}, bf16[8,256,128]{2,1,0:T(8,128)(2,1)S(1)}, bf16[8,256,128]{2,1,0:T(8,128)(2,1)S(1)}, bf16[8,256,128]{2,1,0:T(8,128)(2,1)S(1)}, f32[8,32,256]{2,1,0:T(8,128)S(1)}) custom-call(bf16[256,1024]{1,0:T(8,128)(2,1)} %bitcast.13, bf16[256,1024]{1,0:T(8,128)(2,1)} %bitcast.14, bf16[256,1024]{1,0:T(8,128)(2,1)} %bitcast.15, ...), custom_call_target="tpu_custom_call" | custom-call | tf_op jit(solution)/shard_map/pallas_call | solution.py:512
  67.6 1.8 %shard_map.111 = (bf16[256,2048]{1,0:T(8,128)(2,1)}, bf16[256,1024]{1,0:T(8,128)(2,1)}, bf16[256,1024]{1,0:T(8,128)(2,1)}, bf16[256,1024]{1,0:T(8,128)(2,1)}, f32[32,2048]{1,0:T(8,128)}) custom-call(bf16[256,2048]{1,0:T(8,128)(2,1)S(1)} %get-tuple-element.15.lo, bf16[8,256,128]{2,1,0:T(8,128)(2,1)S(1)} %get-tuple-element.16.qg, ...), custom_call_target="tpu_custom_call" | custom-call | tf_op jit(solution)/shard_map/pallas_call | solution.py:564
Async XLA Ops:
  0.6 0.7 copy-start
  0.6 0.7 copy-start.1

commit v3 on v2

--- a/solution.py
+++ b/solution.py
@@ -38,7 +38,8 @@
 
 
 class Gather:
-    def __init__(self, unit, pos, f, device, send, recv):
+    def __init__(self, unit, pos, f, device, send, recv, direct=False):
+        self.direct = direct
         self.unit = lambda step: unit(lax.rem(pos + step * f + 8, 4))
         self.to = lambda step: device(lax.rem(pos + step * f + 8, 4))
         self.send, self.recv = send, recv
@@ -50,10 +51,13 @@
     def start(self):
         self.copy(0, 0, 1).start()
         self.copy(0, 1, -1).start()
+        if self.direct:
+            self.copy(0, 2, 2).start()
 
     def forward(self):
         self.copy(-1, 0, 1).wait_recv()
-        self.copy(-1, 2, 1).start()
+        if not self.direct:
+            self.copy(-1, 2, 1).start()
 
     def near(self):
         self.copy(1, 1, -1).wait_recv()
@@ -64,7 +68,10 @@
     def drain(self):
         self.copy(0, 0, 1).wait_send()
         self.copy(0, 1, -1).wait_send()
-        self.copy(-1, 2, 1).wait_send()
+        if self.direct:
+            self.copy(0, 2, 2).wait_send()
+        else:
+            self.copy(-1, 2, 1).wait_send()
 
 
 class Scatter:
@@ -144,7 +151,7 @@
     barrier = pltpu.get_barrier_semaphore()
     for step in range(1, 16):
         pl.semaphore_signal(barrier, inc=1, device_id=on_line(lax.rem(line + step, 16)), device_id_type=MESH)
-    for step in (1, 3):
+    for step in range(1, 4):
         pl.semaphore_signal(barrier, inc=1, device_id=on_x(lax.rem(x + step, 4)), device_id_type=MESH)
         pl.semaphore_signal(barrier, inc=1, device_id=on_y(lax.rem(y + step, 4)), device_id_type=MESH)
 
@@ -183,7 +190,7 @@
             mask[pl.ds(i * BLK, BLK), pl.ds(r * BLK, BLK)] = jnp.full((BLK, BLK), fill, F32)
 
     in_w.wait()
-    pl.semaphore_wait(barrier, 19)
+    pl.semaphore_wait(barrier, 21)
 
     wz = rcopy(wb.at[x, zh, y, core], wb.at[x, zh, y, core], wz_s, wz_r, device(x, 7 - z, y, core))
     wz.start()
@@ -192,8 +199,8 @@
         half = zh if s == 0 else 1 - zh
         top, bottom = pl.ds(0, 16), pl.ds(16, 16)
         first = (
-            Gather(lambda p, half=half, top=top: wb.at[x, half, p, core, top], y, f, on_y, ag_s.at[s, 0], ag_r.at[s, 0]),
-            Gather(lambda p, half=half, bottom=bottom: wb.at[p, half, y, core, bottom], x, f, on_x, ag_s.at[s, 1], ag_r.at[s, 1]),
+            Gather(lambda p, half=half, top=top: wb.at[x, half, p, core, top], y, f, on_y, ag_s.at[s, 0], ag_r.at[s, 0], True),
+            Gather(lambda p, half=half, bottom=bottom: wb.at[p, half, y, core, bottom], x, f, on_x, ag_s.at[s, 1], ag_r.at[s, 1], True),
         )
         second = (
             Gather(lambda p, half=half, top=top: wb.at[p, half, :, core, top], x, f, on_x, ag_s.at[s, 2], ag_r.at[s, 2]),
@@ -247,14 +254,13 @@
         in_q[h].wait()
         qrot[h] = rotate(qrot[h].astype(F32), 1).astype(BF16)
 
-    for g in gathers[0][0]:
-        g.forward()
     wz.wait_recv()
     for g in gathers[1][0]:
         g.start()
 
     def second_ring(s):
         for g in gathers[s][0]:
+            g.forward()
             g.near()
             g.far()
         for g in gathers[s][1]:
@@ -284,32 +290,32 @@
             probs[h] = p
             attn[h] = a
 
+        def relay(s):
+            for g in gathers[s][1]:
+                g.forward()
+            send_share(s, -1)
+
+        def near(s):
+            for g in gathers[s][1]:
+                g.near()
+            send_share(s, 1)
+
         @pl.when(i == 0)
         def _():
-            for g in gathers[1][0]:
-                g.forward()
+            second_ring(1)
 
         @pl.when(i == 1)
         def _():
-            second_ring(1)
+            relay(0)
 
         @pl.when(i == 2)
         def _():
-            for g in gathers[0][1]:
-                g.forward()
-            send_share(0, -1)
-            for g in gathers[0][1]:
-                g.near()
-            send_share(0, 1)
+            near(0)
+            relay(1)
 
         @pl.when(i == 3)
         def _():
-            for g in gathers[1][1]:
-                g.forward()
-            send_share(1, -1)
-            for g in gathers[1][1]:
-                g.near()
-            send_share(1, 1)
+            near(1)
 
         for h in heads:
             attn_copy(h).start()
@@ -399,9 +405,12 @@
             for c in give_back(h):
                 c.start()
 
+        @pl.when(i == 1)
+        def _():
+            middle(0, 0)
+
         @pl.when(i == 2)
         def _():
-            middle(0, 0)
             middle(1, 0)
 
         return carry
@@ -417,27 +426,11 @@
         w = wb[:, :, :, j // 4, :, cols].reshape(H * HD, 256)
         lo[:, pl.ds(pl.multiple_of(j * 256, 256), 256)] = dot(rows, w).astype(BF16)
 
-        @pl.when(j == 3)
-        def _():
-            middle(0, 1)
-            middle(1, 1)
-
         return carry
 
-    lax.fori_loop(0, 8, project, 0)
-
-    for s in range(2):
-        for part in range(2):
-            done = scatters[s][2 + part].total().astype(BF16)
-            for j in range(4):
-                zs[s * 4 + j, pl.ds(part * 16, 16)] = done[:, j * 256 : (j + 1) * 256]
-
-    def z_copy(step):
-        to = lax.rem(z + step, 8)
-        return rcopy(zs.at[to], zr.at[step - 1], z_s.at[step - 1], z_r.at[step - 1], device(x, to, y, core))
-
-    for step in range(1, 8):
-        z_copy(step).start()
+    lax.fori_loop(0, 3, project, 0)
+    for s in range(2):
+        middle(s, 1)
 
     def finish(h, carry):
         for c in take_back(h):
@@ -449,12 +442,27 @@
         return carry
 
     lax.fori_loop(0, H, finish, 0)
+
+    for s in range(2):
+        for part in range(2):
+            done = scatters[s][2 + part].total().astype(BF16)
+            for j in range(4):
+                zs[s * 4 + j, pl.ds(part * 16, 16)] = done[:, j * 256 : (j + 1) * 256]
+
+    def z_copy(step):
+        to = lax.rem(z + step, 8)
+        return rcopy(zs.at[to], zr.at[step - 1], z_s.at[step - 1], z_r.at[step - 1], device(x, to, y, core))
+
+    for step in range(1, 8):
+        z_copy(step).start()
+
+    lax.fori_loop(3, 8, project, 0)
     for step in range(1, 8):
         z_copy(step).wait_recv()
     total = zs[z].astype(F32)
     for step in range(7):
         total = total + zr[step].astype(F32)
-    fin[ctx] = total
+    fin[ctx] = total.astype(BF16)
 
     def fin_copy(step):
         to = lax.rem(ctx + step, 8)
@@ -486,17 +494,21 @@
         fin_copy(step).wait_send()
 
 
-def write(lo, qg, kg, vg, fin, lo_hbm, qg_hbm, kg_hbm, vg_hbm, wg_hbm, sem):
-    copies = [(lo, lo_hbm)]
+def write(lo, qg, kg, vg, fin, lo_hbm, qg_hbm, kg_hbm, vg_hbm, wg_hbm, wide, sem):
+    copies = []
+
+    def store(src, dst):
+        copies.append(pltpu.make_async_copy(src, dst, sem.at[len(copies)]))
+        copies[-1].start()
+
+    store(lo, lo_hbm)
     for h in range(H):
         cols = pl.ds(h * HD, HD)
         for src, dst in ((qg, qg_hbm), (kg, kg_hbm), (vg, vg_hbm)):
-            copies.append((src.at[h], dst.at[:, cols]))
+            store(src.at[h], dst.at[:, cols])
+    wide[...] = fin[...].astype(F32)
     for c in range(8):
-        copies.append((fin.at[c], wg_hbm.at[:, pl.ds((c % 2) * HALF + (c // 2) * 256, 256)]))
-    copies = [pltpu.make_async_copy(src, dst, sem.at[i]) for i, (src, dst) in enumerate(copies)]
-    for c in copies:
-        c.start()
+        store(wide.at[c], wg_hbm.at[:, pl.ds((c % 2) * HALF + (c // 2) * 256, 256)])
     for c in copies:
         c.wait()
 
@@ -516,7 +528,7 @@
             V((H, T, HD), BF16),
             V((H, T, HD), BF16),
             V((H, T, HD), BF16),
-            V((8, ROWS, 256), F32),
+            V((8, ROWS, 256), BF16),
         ),
         in_specs=[any_, any_, any_, vmem, smem, any_, any_],
         out_specs=(vmem,) * 5,
@@ -572,7 +584,7 @@
         ),
         in_specs=[vmem] * 5,
         out_specs=(any_,) * 5,
-        scratch_shapes=[dma((33,))],
+        scratch_shapes=[V((8, ROWS, 256), F32), dma((33,))],
         compiler_params=pltpu.CompilerParams(vmem_limit_bytes=LIMIT),
     )(*(pltpu.with_memory_space_constraint(o, pltpu.VMEM) for o in out))
     return lo[None], qg[None], kg[None], vg[None], wg

time: 69.5 us -> 66.9 us (0.963)
  Pallas kernels: 68.1 us -> 65.4 us
    pallas_call x1, Pallas kernels: 66.2 us -> 63.6 us  [shards(): pl.pallas_call(kernel, out_shape=(V((T, D), BF16), V((H, T, HD), BF16), V...]
where the time goes in v3:
time: 66.9 us; the launch traced here: 66.8 us
  Pallas kernels  65.4 us (98%)
  local copies, waits for them, and re-layouts  0.68 us (1%)
    pallas_call x1, Pallas kernels, shards(): pl.pallas_call(kernel, out_shape=(V((T, D), BF16), V((H, T, HD), BF16), V...  63.6 us
    pallas_call x1, Pallas kernels, shards(): pl.pallas_call(write, out_shape=(jax.ShapeDtypeStruct((T, D), BF16), toke...  1.84 us

profile of v3, /device:TPU:1, one launch (start us, length us, event | category | flops | bytes accessed | tf_op | source)
XLA Modules:
  0.0 66.8 jit_solution(15227648370803621090)
XLA Ops:
  0.6 0.0 copy-start
  0.6 0.0 copy-start.1
  0.7 0.7 copy-done
  1.3 0.0 copy-done.1
  1.3 63.6 %shard_map.110 = (bf16[256,2048]{1,0:T(8,128)(2,1)S(1)}, bf16[8,256,128]{2,1,0:T(8,128)(2,1)S(1)}, bf16[8,256,128]{2,1,0:T(8,128)(2,1)S(1)}, bf16[8,256,128]{2,1,0:T(8,128)(2,1)S(1)}, bf16[8,32,256]{2,1,0:T(8,128)(2,1)S(1)}) custom-call(bf16[256,1024]{1,0:T(8,128)(2,1)} %bitcast.13, bf16[256,1024]{1,0:T(8,128)(2,1)} %bitcast.14, bf16[256,1024]{1,0:T(8,128)(2,1)} %bitcast.15, ...), custom_call_target="tpu_custom_call" | custom-call | tf_op jit(solution)/shard_map/pallas_call | solution.py:524
  64.9 1.8 %shard_map.111 = (bf16[256,2048]{1,0:T(8,128)(2,1)}, bf16[256,1024]{1,0:T(8,128)(2,1)}, bf16[256,1024]{1,0:T(8,128)(2,1)}, bf16[256,1024]{1,0:T(8,128)(2,1)}, f32[32,2048]{1,0:T(8,128)}) custom-call(bf16[256,2048]{1,0:T(8,128)(2,1)S(1)} %get-tuple-element.15.lo, bf16[8,256,128]{2,1,0:T(8,128)(2,1)S(1)} %get-tuple-element.16.qg, ...), custom_call_target="tpu_custom_call" | custom-call | tf_op jit(solution)/shard_map/pallas_call | solution.py:576
Async XLA Ops:
  0.6 0.7 %copy-start = (s32[1,16,4]{1,2,0:T(4,128)S(1)}, s32[1,16,4]{1,2,0:T(4,128)}, u32[]{:S(2)}) copy-start(s32[1,16,4]{1,2,0:T(4,128)} %param.11) | copy-start | bytes 772
  0.6 0.7 %copy-start.1 = (s32[1,256]{1,0:T(1,128)S(1)}, s32[1,256]{1,0:T(1,128)}, u32[]{:S(2)}) copy-start(s32[1,256]{1,0:T(1,128)} %tok_ref.1) | copy-start | bytes 3076

commit v4 on v3

--- a/solution.py
+++ b/solution.py
@@ -322,7 +322,8 @@
         return carry
 
     lax.fori_loop(0, H // 2, forward, 0)
-    for s in range(2):
+
+    def far(s):
         for g in gathers[s][1]:
             g.far()
         send_share(s, 2)
@@ -335,7 +336,10 @@
         wg[h // 2, lax.rem(h, 2)] = (term * (1.0 / 32.0)).astype(BF16).reshape(4, ROWS, HALF)
         return carry
 
-    lax.fori_loop(0, H, weight_term, 0)
+    lax.fori_loop(0, 3, weight_term, 0)
+    far(0)
+    lax.fori_loop(3, H, weight_term, 0)
+    far(1)
 
     scatters = []
     for s in range(2):

time: 66.9 us -> 64.6 us (0.966)
  Pallas kernels: 65.4 us -> 63.2 us
    pallas_call x1, Pallas kernels: 63.6 us -> 61.3 us  [shards(): pl.pallas_call(kernel, out_shape=(V((T, D), BF16), V((H, T, HD), BF16), V...]
where the time goes in v4:
time: 64.6 us; the launch traced here: 64.5 us
  Pallas kernels  63.2 us (98%)
  local copies, waits for them, and re-layouts  0.68 us (1%)
  between operations  0.66 us (1%)
    pallas_call x1, Pallas kernels, shards(): pl.pallas_call(kernel, out_shape=(V((T, D), BF16), V((H, T, HD), BF16), V...  61.3 us
    pallas_call x1, Pallas kernels, shards(): pl.pallas_call(write, out_shape=(jax.ShapeDtypeStruct((T, D), BF16), toke...  1.84 us

profile of v4, /device:TPU:1, one launch (start us, length us, event | category | flops | bytes accessed | tf_op | source)
XLA Modules:
  0.0 64.5 jit_solution(17681940121483982013)
XLA Ops:
  0.6 0.0 copy-start
  0.6 0.0 copy-start.1
  0.7 0.7 %copy-done = s32[1,16,4]{1,2,0:T(4,128)S(1)} copy-done((s32[1,16,4]{1,2,0:T(4,128)S(1)}, s32[1,16,4]{1,2,0:T(4,128)}, u32[]{:S(2)}) %copy-start) | copy-done | bytes 280
  1.3 0.0 copy-done.1
  1.3 61.3 %shard_map.110 = (bf16[256,2048]{1,0:T(8,128)(2,1)S(1)}, bf16[8,256,128]{2,1,0:T(8,128)(2,1)S(1)}, bf16[8,256,128]{2,1,0:T(8,128)(2,1)S(1)}, bf16[8,256,128]{2,1,0:T(8,128)(2,1)S(1)}, bf16[8,32,256]{2,1,0:T(8,128)(2,1)S(1)}) custom-call(bf16[256,1024]{1,0:T(8,128)(2,1)} %bitcast.13, bf16[256,1024]{1,0:T(8,128)(2,1)} %bitcast.14, bf16[256,1024]{1,0:T(8,128)(2,1)} %bitcast.15, ...), custom_call_target="tpu_custom_call" | custom-call | tf_op jit(solution)/shard_map/pallas_call | solution.py:528
  62.7 1.8 %shard_map.111 = (bf16[256,2048]{1,0:T(8,128)(2,1)}, bf16[256,1024]{1,0:T(8,128)(2,1)}, bf16[256,1024]{1,0:T(8,128)(2,1)}, bf16[256,1024]{1,0:T(8,128)(2,1)}, f32[32,2048]{1,0:T(8,128)}) custom-call(bf16[256,2048]{1,0:T(8,128)(2,1)S(1)} %get-tuple-element.15.lo, bf16[8,256,128]{2,1,0:T(8,128)(2,1)S(1)} %get-tuple-element.16.qg, ...), custom_call_target="tpu_custom_call" | custom-call | tf_op jit(solution)/shard_map/pallas_call | solution.py:580
Async XLA Ops:
  0.6 0.7 %copy-start = (s32[1,16,4]{1,2,0:T(4,128)S(1)}, s32[1,16,4]{1,2,0:T(4,128)}, u32[]{:S(2)}) copy-start(s32[1,16,4]{1,2,0:T(4,128)} %param.11) | copy-start | bytes 772
  0.6 0.7 %copy-start.1 = (s32[1,256]{1,0:T(1,128)S(1)}, s32[1,256]{1,0:T(1,128)}, u32[]{:S(2)}) copy-start(s32[1,256]{1,0:T(1,128)} %tok_ref.1) | copy-start | bytes 3076
